TPU v7x, 256 devices: a whole 4x4x8 slice. The times are simulated.
256 devices in a mesh: copy: 2 (over y_hi), dp: 8 (over x, core), fsdp: 16 (over y_lo, z).
Axes of the slice: x: 4, y: 4 (y_hi: 2, y_lo: 2; y = y_hi * 2 + y_lo), z: 8, core: 2. Of those that a mesh axis runs over, the one named last changes fastest.
Arguments:
- queries: bfloat16 [2, 128, 256, 2560], P('copy', ('dp', 'fsdp')), may hold values from -25 to 25
- keys: bfloat16 [2, 128, 256, 2560], P('copy', ('dp', 'fsdp')), may hold values from -25 to 25
- values: bfloat16 [2, 128, 256, 2560], P('copy', ('dp', 'fsdp')), may hold values from -6 to 6
- residual: bfloat16 [2, 128, 256, 2560], P('copy', ('dp', 'fsdp')), may hold values from -6 to 6
- event_ids: int32 [128, 256], P(('dp', 'fsdp')), may hold values from 0 to 1023
- lengths: int32 [128], replicated, may hold values from 8 to 256, as said below
- type_weight: float32 [1024], replicated, may hold values from 0.25 to 4
- w_out: bfloat16 [2, 2560, 2560], P('copy', 'fsdp'), may hold values from -0.125 to 0.125
- gain: float32 [2, 2560], P('copy'), may hold values from 0.5 to 1.5
Outputs:
- loss: float32 [2, 128], P('copy', ('dp', 'fsdp'))
- d_queries: bfloat16 [2, 128, 256, 2560], P('copy', ('dp', 'fsdp'))
- d_keys: bfloat16 [2, 128, 256, 2560], P('copy', ('dp', 'fsdp'))
- d_values: bfloat16 [2, 128, 256, 2560], P('copy', ('dp', 'fsdp'))
- d_wo: float32 [2, 2560, 2560], P('copy', 'fsdp')
Inputs may be any that keep to these rules, and one draw needn't show every extreme that they name: `lengths`: every history has at least 8 valid events and some history has all 256.
All inputs are finite; a program needn't handle non-finite values.
Results may differ from a plain program's by a relative error of at most 0.02.
Values may be sent and summed in bfloat16 or wider, within the bound.
A program may use at most 128 MiB of HBM per device.

v0:
```python
import jax
import jax.numpy as jnp
from jax import lax
from jax.sharding import PartitionSpec as P

DH = 128


def partner_2(value, axis, bit):
    return lax.ppermute(value, axis, [(i, i ^ 1 << bit) for i in range(lax.axis_size(axis))])


def body(queries, keys, values, residual, event_ids, lengths, type_weight, w_out, gain):
    seq = queries.shape[2]
    heads_width = queries.shape[3]
    width = residual.shape[3]
    head_size = DH
    heads = heads_width // head_size
    own = lax.axis_index(("dp", "fsdp"))
    length = lengths[own]
    count = jnp.sum(lengths).astype(jnp.float32)
    my_gain = gain[0]
    full_weight = lax.all_gather(w_out[0], "fsdp", axis=0, tiled=True)
    arrange = lambda matrix: matrix
    restore = lambda matrix: matrix
    query_heads = queries[0, 0].reshape(seq, heads, head_size)
    key_heads = keys[0, 0].reshape(seq, heads, head_size)
    value_heads = values[0, 0].reshape(seq, heads, head_size)
    scale = jnp.sqrt(jnp.float32(head_size))
    scores = (
        jnp.einsum("qhd,khd->hqk", query_heads, key_heads, preferred_element_type=jnp.float32)
        / scale
    )
    rows = jnp.arange(seq, dtype=jnp.int32)[:, None]
    cols = jnp.arange(seq, dtype=jnp.int32)[None, :]
    valid = (cols <= rows) & (cols < length)
    scores = jnp.where(valid[None], scores, jnp.float32(-1e30))
    probs = jax.nn.softmax(scores, axis=-1)
    probs_b = probs.astype(jnp.bfloat16)
    attn = (
        jnp.einsum("hqk,khd->qhd", probs_b, value_heads, preferred_element_type=jnp.float32)
        .reshape(seq, heads_width)
        .astype(jnp.bfloat16)
    )
    hidden = residual[0, 0].astype(jnp.float32) + jnp.dot(
        arrange(attn), full_weight, preferred_element_type=jnp.float32
    )
    inv = lax.rsqrt(jnp.mean(hidden * hidden, axis=-1, keepdims=True) + 1e-06)
    normed = hidden * inv
    feat = normed * my_gain[None, :]
    partner = partner_2(feat.astype(jnp.bfloat16), "copy", 0)
    type_count = type_weight.shape[0]
    matches = event_ids[0][:, None] == jnp.arange(type_count, dtype=jnp.int32)[None, :]
    looked_up = jnp.sum(jnp.where(matches, type_weight[None, :], jnp.float32(0.0)), axis=-1)
    live = jnp.arange(seq, dtype=jnp.int32) < length
    tok_w = jnp.where(live, looked_up, jnp.float32(0.0))
    diff = feat - partner.astype(jnp.float32)
    loss = jnp.sum(tok_w * jnp.sum(diff * diff, axis=-1)) / (width * count)
    dfeat = 2.0 * tok_w[:, None] * diff / (width * count)
    scaled = dfeat * my_gain[None, :]
    d_hidden = (inv * (scaled - normed * jnp.mean(normed * scaled, axis=-1, keepdims=True))).astype(
        jnp.bfloat16
    )
    partial_term = jnp.dot(attn.T, d_hidden, preferred_element_type=jnp.float32).astype(
        jnp.bfloat16
    )
    row_sum = lax.psum_scatter(partial_term, "fsdp", scatter_dimension=0, tiled=True).astype(
        jnp.float32
    )
    d_wo = lax.psum(row_sum.astype(jnp.bfloat16), "dp").astype(jnp.float32)
    d_attn_arranged = lax.dot_general(
        d_hidden, full_weight, (((1,), (1,)), ((), ())), preferred_element_type=jnp.float32
    )
    d_attn = restore(d_attn_arranged).astype(jnp.bfloat16)
    d_heads = d_attn.reshape(seq, heads, head_size)
    d_values = (
        jnp.einsum("hqk,qhd->khd", probs_b, d_heads, preferred_element_type=jnp.float32)
        .reshape(seq, heads_width)
        .astype(jnp.bfloat16)
    )
    dprob = jnp.einsum("qhd,khd->hqk", d_heads, value_heads, preferred_element_type=jnp.float32)
    delta = jnp.sum(dprob * probs, axis=-1, keepdims=True)
    ds = (probs * (dprob - delta) / scale).astype(jnp.bfloat16)
    d_queries = (
        jnp.einsum("hqk,khd->qhd", ds, key_heads, preferred_element_type=jnp.float32)
        .reshape(seq, heads_width)
        .astype(jnp.bfloat16)
    )
    d_keys = (
        jnp.einsum("hqk,qhd->khd", ds, query_heads, preferred_element_type=jnp.float32)
        .reshape(seq, heads_width)
        .astype(jnp.bfloat16)
    )
    return (
        loss.reshape(1, 1),
        d_queries[None, None],
        d_keys[None, None],
        d_values[None, None],
        d_wo[None],
    )


def solution(mesh):
    in_specs = (
        P("copy", ("dp", "fsdp"), None, None),
        P("copy", ("dp", "fsdp"), None, None),
        P("copy", ("dp", "fsdp"), None, None),
        P("copy", ("dp", "fsdp"), None, None),
        P(("dp", "fsdp"), None),
        P(),
        P(),
        P("copy", "fsdp", None),
        P("copy", None),
    )
    out_specs = (
        P("copy", ("dp", "fsdp")),
        P("copy", ("dp", "fsdp"), None, None),
        P("copy", ("dp", "fsdp"), None, None),
        P("copy", ("dp", "fsdp"), None, None),
        P("copy", "fsdp", None),
    )
    return jax.shard_map(body, mesh=mesh, in_specs=in_specs, out_specs=out_specs, check_vma=False)
```

profile of v0, /device:TPU:8, one launch (start us, length us, event | category | flops | bytes accessed | tf_op | source)
XLA Modules:
  0.0 438.8 jit_solution(15980191786920070180)
XLA Ops:
  7.2 0.0 copy-start.3
  7.2 0.0 all-gather.3.cloned.1.call-start
  7.2 0.7 all-gather.3.cloned.1.call-update
  7.9 0.0 reduce-scatter.2.cloned.1.call-start
  8.0 1.6 copy.48
  9.6 0.0 copy-start
  9.6 0.0 copy-done.3
  9.6 0.0 copy-start.9
  9.6 0.0 copy-start.6
  9.6 1.4 copy.44
  11.1 2.5 copy.45
  13.6 0.0 copy-done.9
  13.6 0.6 dynamic_slice.3
  14.2 0.0 copy-done.6
  14.2 0.7 iota_compare_fusion.2
  14.9 0.1 fusion.35
  15.0 5.6 %fusion.44 = (f32[20,256]{1,0:T(8,128)S(1)}, f32[20,256,256]{1,2,0:T(8,128)}) fusion(pred[256,256]{0,1:T(8,128)(4,1)S(1)} %fusion.35, bf16[256,20,128]{0,2,1:T(8,128)(2,1)S(1)} %bitcast.52, bf16[256,20,128]{0,2,1:T(8,128)(2,1)} %bitcast.54), kind=kOutput, calls=%fused_computation.52 | convolution fusion | flops 340787456 | bytes 7950336 | tf_op jit(solution)/shard_map/sub | solution.py:38
  20.6 4.1 convolution_convert_fusion.1
  24.7 135.4 %all-gather.3.cloned.1.call-done = bf16[1,2560,2560]{2,1,0:T(8,128)(2,1)} async-done(((bf16[1,160,2560]{2,1,0:T(8,128)(2,1)}), bf16[1,2560,2560]{2,1,0:T(8,128)(2,1)}) %all-gather.3.cloned.1.call-update) | async-done | bytes 13107216 | tf_op jit(solution)/shard_map/all_gather | solution.py:23
  160.1 9.2 %multiply_reduce_fusion.3 = (f32[256]{0:T(256)S(1)}, f32[256,2560]{1,0:T(8,128)S(1)}) fusion(bf16[256,2560]{0,1:T(8,128)(2,1)} %bitcast.50, bf16[1,2560,2560]{2,1,0:T(8,128)(2,1)} %all-gather.3.cloned.1.call-done, bf16[1,1,256,2560]{3,2,1,0:T(8,128)(2,1)} %param.12), kind=kOutput, calls=%fused_computation.22 | convolution fusion | flops 3358064384 | bytes 18351104 | tf_op jit(solution)/shard_map/dot_general | solution.py:45
  169.2 0.0 copy-start.7
  169.3 0.0 copy-start.8
  169.3 1.3 multiply_convert_fusion.2
  170.6 2.4 collective-permute-start
  173.0 0.7 reduce_sum.77
  174.3 0.0 copy-start.2
  174.3 0.2 select_reduce_fusion
  174.6 0.8 select_multiply_fusion
  175.4 27.4 %collective-permute-done = bf16[256,2560]{1,0:T(8,128)(2,1)} collective-permute-done((bf16[256,2560]{1,0:T(8,128)(2,1)}, bf16[256,2560]{1,0:T(8,128)(2,1)}, u32[]{:S(2)}, u32[]{:S(2)}) %collective-permute-start) | collective-permute-done | bytes 1310752 | tf_op jit(solution)/shard_map/ppermute | solution.py:10
  202.8 2.4 multiply_reduce_fusion.1
  205.3 8.6 %convolution_convert_fusion = bf16[2560,2560]{1,0:T(8,128)(2,1)} fusion(bf16[256,2560]{0,1:T(8,128)(2,1)S(1)} %bitcast.51, f32[256,2560]{1,0:T(8,128)S(1)} %get-tuple-element.25, bf16[256,2560]{1,0:T(8,128)(2,1)} %collective-permute-done, f32[256]{0:T(256)S(1)} %broadcast_multiply_fusion, f32[]{:T(128)S(6)} %mul.91, f32[256]{0:T(256)S(1)} %select_multiply_fusion, ...), kind=kOutput, calls=%fused_computation.2 | convolution fusion | flops 3369205760 | bytes 18363396 | tf_op jit(solution)/shard_map/dot_general | solution.py:64
  213.9 0.0 reduce-scatter.2.cloned.1.call-update
  213.9 0.2 all-reduce.2.cloned.1.call-start
  214.1 1.2 multiply_reduce_fusion.4
  216.0 10.0 %fusion.11 = bf16[256,2560]{1,0:T(8,128)(2,1)} fusion(bf16[1,2560,2560]{2,1,0:T(8,128)(2,1)} %all-gather.3.cloned.1.call-done, f32[256,2560]{1,0:T(8,128)S(1)} %get-tuple-element.25, bf16[256,2560]{1,0:T(8,128)(2,1)} %collective-permute-done, f32[256]{0:T(256)S(1)} %broadcast_multiply_fusion, f32[]{:T(128)S(6)} %mul.91, f32[256]{0:T(256)S(1)} %select_multiply_fusion, ...), kind=kOutput, calls=%fused_computation.14 | convolution fusion | flops 3363307520 | bytes 18363396 | tf_op jit(solution)/shard_map/dot_general | solution.py:71
  226.1 1.7 copy.50
  227.8 0.0 copy-done.1
  227.8 3.2 fusion.45
  231.0 10.4 %fusion.27 = bf16[20,256,128]{1,2,0:T(8,128)(2,1)} fusion(bf16[256,20,128]{0,2,1:T(8,128)(2,1)} %bitcast.55, f32[20,256,256]{1,2,0:T(8,128)} %fusion.45, f32[20,256,256]{1,2,0:T(8,128)} %get-tuple-element.23, f32[20,256]{1,0:T(8,128)S(1)} %get-tuple-element.22), kind=kOutput, calls=%fused_computation.30 | convolution fusion | flops 345380096 | bytes 13127680 | tf_op jit(solution)/shard_map/hqk,khd->qhd/dot_general | solution.py:85
  241.4 2.5 copy.56
  243.9 10.1 %fusion.30 = bf16[20,256,128]{1,2,0:T(8,128)(2,1)} fusion(bf16[256,20,128]{0,2,1:T(8,128)(2,1)S(1)} %bitcast.53, f32[20,256,256]{1,2,0:T(8,128)} %fusion.45, f32[20,256,256]{1,2,0:T(8,128)} %get-tuple-element.23, f32[20,256]{1,0:T(8,128)S(1)} %get-tuple-element.22), kind=kOutput, calls=%fused_computation.31 | convolution fusion | flops 345380096 | bytes 13127680 | tf_op jit(solution)/shard_map/hqk,qhd->khd/dot_general | solution.py:90
  254.0 2.4 copy.57
  256.4 104.1 %reduce-scatter.2.cloned.1.call-done = bf16[160,2560]{1,0:T(8,128)(2,1)} async-done(((bf16[2560,2560]{1,0:T(8,128)(2,1)}), bf16[160,2560]{1,0:T(8,128)(2,1)}) %reduce-scatter.2.cloned.1.call-update) | async-done | bytes 819216 | tf_op jit(solution)/shard_map/reduce_scatter | solution.py:67
  360.5 0.0 all-reduce.2.cloned.1.call-update
  360.5 3.5 convolution_convert_fusion.2
  364.0 1.6 copy.58
  365.6 63.0 %all-reduce.2.cloned.1.call-done = bf16[1,160,2560]{2,1,0:T(8,128)(2,1)} async-done(((bf16[1,160,2560]{2,1,0:T(8,128)(2,1)}), bf16[1,160,2560]{2,1,0:T(8,128)(2,1)}) %all-reduce.2.cloned.1.call-update) | async-done | bytes 819216 | tf_op jit(solution)/shard_map/psum | solution.py:70
  428.6 2.5 broadcast_in_dim.54
  (12 shorter events, 0.1 us)
Async XLA Ops:
  7.2 2.4 copy-start.3
  7.2 152.9 %all-gather.3.cloned.1.call-start = ((), (), s32[]{:S(2)}) async-start(), calls=%async_computation.3 | async-start | bytes 13926400 | tf_op jit(solution)/shard_map/all_gather | solution.py:23
  7.9 352.6 %reduce-scatter.2.cloned.1.call-start = ((), (), s32[]{:S(2)}) async-start(), calls=%async_computation.1 | async-start | bytes 13926400 | tf_op jit(solution)/shard_map/reduce_scatter | solution.py:67
  9.6 11.0 %copy-start = (bf16[1,1,256,2560]{2,3,1,0:T(8,128)(2,1)}, bf16[1,1,256,2560]{2,3,1,0:T(8,128)(2,1)S(1)}, u32[]{:S(2)}) copy-start(bf16[1,1,256,2560]{2,3,1,0:T(8,128)(2,1)S(1)} %copy.48) | copy-start | bytes 3932164
  9.6 4.0 copy-start.9
  9.6 4.6 %copy-start.6 = (f32[1,2560]{1,0:T(1,128)S(1)}, f32[1,2560]{1,0:T(1,128)}, u32[]{:S(2)}) copy-start(f32[1,2560]{1,0:T(1,128)} %param.17) | copy-start | bytes 30724
  11.1 3.9 copy-start.4
  169.2 5.1 %copy-start.7 = (f32[1024]{0:T(1024)S(1)}, f32[1024]{0:T(1024)}, u32[]{:S(2)}) copy-start(f32[1024]{0:T(1024)} %param.15) | copy-start | bytes 12292
  169.3 5.1 %copy-start.8 = (s32[1,256]{1,0:T(1,128)S(1)}, s32[1,256]{1,0:T(1,128)}, u32[]{:S(2)}) copy-start(s32[1,256]{1,0:T(1,128)} %param.13) | copy-start | bytes 3076
  170.6 32.2 %collective-permute-start = (bf16[256,2560]{1,0:T(8,128)(2,1)}, bf16[256,2560]{1,0:T(8,128)(2,1)}, u32[]{:S(2)}, u32[]{:S(2)}) collective-permute-start(bf16[256,2560]{1,0:T(8,128)(2,1)} %multiply_convert_fusion.2), channel_id=1, source_target_pairs={{0,128},{128,0},{1,129},{129,1},{2,130},{130,2},{3,131},{131,3},{4... | collective-permute-start | bytes 3932168 | tf_op jit(solution)/shard_map/ppermute | solution.py:10
  174.3 30.9 %copy-start.2 = (bf16[20,256,128]{1,2,0:T(8,128)(2,1)S(1)}, bf16[20,256,128]{1,2,0:T(8,128)(2,1)}, u32[]{:S(2)}) copy-start(bf16[20,256,128]{1,2,0:T(8,128)(2,1)} %convolution_convert_fusion.1) | copy-start | bytes 3932164
  213.9 214.7 %all-reduce.2.cloned.1.call-start = ((), (), s32[]{:S(2)}) async-start(), calls=%async_computation.2 | async-start | bytes 1638400 | tf_op jit(solution)/shard_map/psum | solution.py:70
  226.1 1.7 copy-start.1
  241.4 2.5 copy-start.5
Sparse Core Ops, SparseCore 0:
  9.8 150.2 all-gather.2
  214.0 146.4 reduce-scatter.1
  362.9 65.7 all-reduce.1
where the time goes:
time: 439 us
  waiting for transfers between devices  331 us (75%)
  matrix products  64.6 us (15%)
  between operations  16.3 us (4%)
  local copies, waits for them, and re-layouts  14.4 us (3%)
  other arithmetic  9.98 us (2%)
    all_gather x1, waiting for transfers between devices, body(): full_weight = lax.all_gather(w_out[0], 'fsdp', axis=0, tiled=True)  135 us
    reduce_scatter x1, waiting for transfers between devices, body(): lax.psum_scatter(partial_term, 'fsdp', scatter_dimension=0, tiled=True)  104 us
    psum x1, waiting for transfers between devices, body(): d_wo = lax.psum(row_sum.astype(jnp.bfloat16), 'dp').astype(jnp.float32)  63 us
    ppermute x1, waiting for transfers between devices, partner_2(): lax.ppermute(value, axis, [(i, i ^ 1 << bit) for i in range(lax.axis_size...  27.4 us
    unnamed x26, local copies, waits for them, and re-layouts  12.1 us
    dot_general x1, matrix products, body(): jnp.einsum('hqk,khd->qhd', ds, key_heads, preferred_element_type=jnp.floa...  10.4 us
    dot_general x1, matrix products, body(): jnp.einsum('hqk,qhd->khd', ds, query_heads, preferred_element_type=jnp.fl...  10.1 us
    dot_general x1, matrix products, body(): lax.dot_general(d_hidden, full_weight, (((1,), (1,)), ((), ())), preferre...  10 us
  transfers between devices with their start and end apart: 4, of which 4 were waited for; matrix products, arithmetic and copies ran while one was open for 15% of the time, Pallas kernels for 0%

commit v1 on v0

--- a/solution.py
+++ b/solution.py
@@ -67,7 +67,7 @@
     row_sum = lax.psum_scatter(partial_term, "fsdp", scatter_dimension=0, tiled=True).astype(
         jnp.float32
     )
-    d_wo = lax.psum(row_sum.astype(jnp.bfloat16), "dp").astype(jnp.float32)
+    d_wo = jnp.sum(lax.all_gather(row_sum.astype(jnp.bfloat16), "dp"), axis=0).astype(jnp.float32)
     d_attn_arranged = lax.dot_general(
         d_hidden, full_weight, (((1,), (1,)), ((), ())), preferred_element_type=jnp.float32
     )

time: 439 us -> 424 us (0.966)
  waiting for transfers between devices: 331 us -> 310 us
    psum x1 -> x0, waiting for transfers between devices: 63 us -> none  [body(): d_wo = lax.psum(row_sum.astype(jnp.bfloat16), 'dp').astype(jnp.float32)]
    reduce_scatter x1, waiting for transfers between devices: 104 us -> 146 us  [body(): lax.psum_scatter(partial_term, 'fsdp', scatter_dimension=0, tiled=True)]
  transfers between devices with their start and end apart: 4 -> 4, of which waited for: 4 -> 3; matrix products, arithmetic and copies ran while one was open for 15% -> 15% of each run, Pallas kernels for 0% -> 0%
where the time goes in v1:
time: 424 us; the launch traced here: 422 us
  waiting for transfers between devices  310 us (73%)
  matrix products  64.9 us (15%)
  between operations  16.3 us (4%)
  local copies, waits for them, and re-layouts  14.7 us (3%)
  other arithmetic  13 us (3%)
    reduce_scatter x1, waiting for transfers between devices, body(): lax.psum_scatter(partial_term, 'fsdp', scatter_dimension=0, tiled=True)  146 us
    all_gather x1, waiting for transfers between devices, body(): full_weight = lax.all_gather(w_out[0], 'fsdp', axis=0, tiled=True)  135 us
    ppermute x1, waiting for transfers between devices, partner_2(): lax.ppermute(value, axis, [(i, i ^ 1 << bit) for i in range(lax.axis_size...  27.4 us
    unnamed x26, local copies, waits for them, and re-layouts  12.3 us
    dot_general x1, matrix products, body(): jnp.einsum('hqk,khd->qhd', ds, key_heads, preferred_element_type=jnp.floa...  10.4 us
    dot_general x1, matrix products, body(): jnp.einsum('hqk,qhd->khd', ds, query_heads, preferred_element_type=jnp.fl...  10.3 us
    dot_general x1, matrix products, body(): lax.dot_general(d_hidden, full_weight, (((1,), (1,)), ((), ())), preferre...  10 us
    dot_general x1, matrix products, body(): jnp.dot(arrange(attn), full_weight, preferred_element_type=jnp.float32)  9.16 us
  transfers between devices with their start and end apart: 4, of which 3 were waited for; matrix products, arithmetic and copies ran while one was open for 15% of the time, Pallas kernels for 0%

profile of v1, /device:TPU:8, one launch (start us, length us, event | category | flops | bytes accessed | tf_op | source)
XLA Modules:
  0.0 421.6 jit_solution(4373585531279610610)
XLA Ops:
  7.2 0.0 copy-start.3
  7.2 0.0 all-gather.5.cloned.1.call-start
  7.2 0.7 all-gather.5.cloned.1.call-update
  7.9 0.0 reduce-scatter.2.cloned.1.call-start
  8.0 1.6 copy.48
  9.6 0.0 copy-start
  9.6 0.0 copy-done.3
  9.6 0.0 copy-start.9
  9.6 0.0 copy-start.6
  9.6 1.4 copy.44
  11.1 2.5 copy.45
  13.6 0.0 copy-done.9
  13.6 0.6 dynamic_slice.3
  14.2 0.0 copy-done.6
  14.2 0.7 iota_compare_fusion.2
  14.9 0.1 fusion.35
  15.0 5.6 %fusion.44 = (f32[20,256]{1,0:T(8,128)S(1)}, f32[20,256,256]{1,2,0:T(8,128)}) fusion(pred[256,256]{0,1:T(8,128)(4,1)S(1)} %fusion.35, bf16[256,20,128]{0,2,1:T(8,128)(2,1)S(1)} %bitcast.56, bf16[256,20,128]{0,2,1:T(8,128)(2,1)} %bitcast.58), kind=kOutput, calls=%fused_computation.53 | convolution fusion | flops 340787456 | bytes 7950336 | tf_op jit(solution)/shard_map/sub | solution.py:38
  20.6 4.1 convolution_convert_fusion.1
  24.7 135.4 %all-gather.5.cloned.1.call-done = bf16[1,2560,2560]{2,1,0:T(8,128)(2,1)} async-done(((bf16[1,160,2560]{2,1,0:T(8,128)(2,1)}), bf16[1,2560,2560]{2,1,0:T(8,128)(2,1)}) %all-gather.5.cloned.1.call-update) | async-done | bytes 13107216 | tf_op jit(solution)/shard_map/all_gather | solution.py:23
  160.1 9.2 %multiply_reduce_fusion.3 = (f32[256]{0:T(256)S(1)}, f32[256,2560]{1,0:T(8,128)S(1)}) fusion(bf16[256,2560]{0,1:T(8,128)(2,1)} %bitcast.54, bf16[1,2560,2560]{2,1,0:T(8,128)(2,1)} %all-gather.5.cloned.1.call-done, bf16[1,1,256,2560]{3,2,1,0:T(8,128)(2,1)} %param.12), kind=kOutput, calls=%fused_computation.22 | convolution fusion | flops 3358064384 | bytes 18351104 | tf_op jit(solution)/shard_map/dot_general | solution.py:45
  169.2 0.0 copy-start.7
  169.3 0.0 copy-start.8
  169.3 1.3 multiply_convert_fusion.2
  170.6 2.4 collective-permute-start
  173.0 0.7 reduce_sum.89
  174.3 0.0 copy-start.2
  174.3 0.2 select_reduce_fusion
  174.6 0.8 select_multiply_fusion
  175.4 27.4 %collective-permute-done = bf16[256,2560]{1,0:T(8,128)(2,1)} collective-permute-done((bf16[256,2560]{1,0:T(8,128)(2,1)}, bf16[256,2560]{1,0:T(8,128)(2,1)}, u32[]{:S(2)}, u32[]{:S(2)}) %collective-permute-start) | collective-permute-done | bytes 1310752 | tf_op jit(solution)/shard_map/ppermute | solution.py:10
  202.8 2.4 multiply_reduce_fusion.1
  205.3 8.6 %convolution_convert_fusion = bf16[2560,2560]{1,0:T(8,128)(2,1)} fusion(bf16[256,2560]{0,1:T(8,128)(2,1)S(1)} %bitcast.55, f32[256,2560]{1,0:T(8,128)S(1)} %get-tuple-element.25, bf16[256,2560]{1,0:T(8,128)(2,1)} %collective-permute-done, f32[256]{0:T(256)S(1)} %broadcast_multiply_fusion, f32[]{:T(128)S(6)} %mul.91, f32[256]{0:T(256)S(1)} %select_multiply_fusion, ...), kind=kOutput, calls=%fused_computation.2 | convolution fusion | flops 3369205760 | bytes 18363396 | tf_op jit(solution)/shard_map/dot_general | solution.py:64
  213.9 0.0 reduce-scatter.2.cloned.1.call-update
  213.9 0.2 all-gather.7.cloned.1.call-start
  214.1 146.4 %reduce-scatter.2.cloned.1.call-done = bf16[160,2560]{1,0:T(8,128)(2,1)} async-done(((bf16[2560,2560]{1,0:T(8,128)(2,1)}), bf16[160,2560]{1,0:T(8,128)(2,1)}) %reduce-scatter.2.cloned.1.call-update) | async-done | bytes 819216 | tf_op jit(solution)/shard_map/reduce_scatter | solution.py:67
  360.5 0.0 all-gather.7.cloned.1.call-update
  360.5 1.2 multiply_reduce_fusion.4
  362.4 10.0 %fusion.11 = bf16[256,2560]{1,0:T(8,128)(2,1)} fusion(bf16[1,2560,2560]{2,1,0:T(8,128)(2,1)} %all-gather.5.cloned.1.call-done, f32[256,2560]{1,0:T(8,128)S(1)} %get-tuple-element.25, bf16[256,2560]{1,0:T(8,128)(2,1)} %collective-permute-done, f32[256]{0:T(256)S(1)} %broadcast_multiply_fusion, f32[]{:T(128)S(6)} %mul.91, f32[256]{0:T(256)S(1)} %select_multiply_fusion, ...), kind=kOutput, calls=%fused_computation.14 | convolution fusion | flops 3363307520 | bytes 18363396 | tf_op jit(solution)/shard_map/dot_general | solution.py:71
  372.5 1.8 copy.50
  374.2 0.2 copy-done.1
  374.4 3.2 fusion.45
  377.6 10.4 %fusion.27 = bf16[20,256,128]{1,2,0:T(8,128)(2,1)} fusion(bf16[256,20,128]{0,2,1:T(8,128)(2,1)} %bitcast.59, f32[20,256,256]{1,2,0:T(8,128)} %fusion.45, f32[20,256,256]{1,2,0:T(8,128)} %get-tuple-element.23, f32[20,256]{1,0:T(8,128)S(1)} %get-tuple-element.22), kind=kOutput, calls=%fused_computation.30 | convolution fusion | flops 345380096 | bytes 13127680 | tf_op jit(solution)/shard_map/hqk,khd->qhd/dot_general | solution.py:85
  388.0 2.5 copy.56
  390.5 10.3 %fusion.30 = bf16[20,256,128]{1,2,0:T(8,128)(2,1)} fusion(bf16[256,20,128]{0,2,1:T(8,128)(2,1)S(1)} %bitcast.57, f32[20,256,256]{1,2,0:T(8,128)} %fusion.45, f32[20,256,256]{1,2,0:T(8,128)} %get-tuple-element.23, f32[20,256]{1,0:T(8,128)S(1)} %get-tuple-element.22), kind=kOutput, calls=%fused_computation.31 | convolution fusion | flops 345380096 | bytes 13127680 | tf_op jit(solution)/shard_map/hqk,qhd->khd/dot_general | solution.py:90
  400.8 2.4 copy.57
  403.3 3.6 convolution_convert_fusion.2
  406.8 1.6 copy.58
  408.4 4.2 reduce_sum.92
  412.6 1.3 bitcast_convert_fusion
  (13 shorter events, 0.1 us)
Async XLA Ops:
  7.2 2.4 copy-start.3
  7.2 152.9 %all-gather.5.cloned.1.call-start = ((), (), s32[]{:S(2)}) async-start(), calls=%async_computation.2 | async-start | bytes 13926400 | tf_op jit(solution)/shard_map/all_gather | solution.py:23
  7.9 352.6 %reduce-scatter.2.cloned.1.call-start = ((), (), s32[]{:S(2)}) async-start(), calls=%async_computation.1 | async-start | bytes 13926400 | tf_op jit(solution)/shard_map/reduce_scatter | solution.py:67
  9.6 11.0 %copy-start = (bf16[1,1,256,2560]{2,3,1,0:T(8,128)(2,1)}, bf16[1,1,256,2560]{2,3,1,0:T(8,128)(2,1)S(1)}, u32[]{:S(2)}) copy-start(bf16[1,1,256,2560]{2,3,1,0:T(8,128)(2,1)S(1)} %copy.48) | copy-start | bytes 3932164
  9.6 4.0 copy-start.9
  9.6 4.6 %copy-start.6 = (f32[1,2560]{1,0:T(1,128)S(1)}, f32[1,2560]{1,0:T(1,128)}, u32[]{:S(2)}) copy-start(f32[1,2560]{1,0:T(1,128)} %param.17) | copy-start | bytes 30724
  11.1 3.9 copy-start.4
  169.2 5.1 %copy-start.7 = (f32[1024]{0:T(1024)S(1)}, f32[1024]{0:T(1024)}, u32[]{:S(2)}) copy-start(f32[1024]{0:T(1024)} %param.15) | copy-start | bytes 12292
  169.3 5.1 %copy-start.8 = (s32[1,256]{1,0:T(1,128)S(1)}, s32[1,256]{1,0:T(1,128)}, u32[]{:S(2)}) copy-start(s32[1,256]{1,0:T(1,128)} %param.13) | copy-start | bytes 3076
  170.6 32.2 %collective-permute-start = (bf16[256,2560]{1,0:T(8,128)(2,1)}, bf16[256,2560]{1,0:T(8,128)(2,1)}, u32[]{:S(2)}, u32[]{:S(2)}) collective-permute-start(bf16[256,2560]{1,0:T(8,128)(2,1)} %multiply_convert_fusion.2), channel_id=1, source_target_pairs={{0,128},{128,0},{1,129},{129,1},{2,130},{130,2},{3,131},{131,3},{4... | collective-permute-start | bytes 3932168 | tf_op jit(solution)/shard_map/ppermute | solution.py:10
  174.3 30.9 %copy-start.2 = (bf16[20,256,128]{1,2,0:T(8,128)(2,1)S(1)}, bf16[20,256,128]{1,2,0:T(8,128)(2,1)}, u32[]{:S(2)}) copy-start(bf16[20,256,128]{1,2,0:T(8,128)(2,1)} %convolution_convert_fusion.1) | copy-start | bytes 3932164
  213.9 194.5 %all-gather.7.cloned.1.call-start = ((), (), s32[]{:S(2)}) async-start(), calls=%async_computation.3 | async-start | bytes 7372800 | tf_op jit(solution)/shard_map/all_gather | solution.py:70
  372.5 2.0 copy-start.1
  388.0 2.5 copy-start.5
Sparse Core Ops, SparseCore 0:
  9.8 150.2 all-gather.4
  214.0 146.4 reduce-scatter.1
  362.3 43.1 all-gather.6
